TPU v7x, 32 devices: a whole 2x2x4 slice. The times are simulated.
32 devices in a mesh: section: 2 (over x), kvp: 16 (over z, y, core).
Axes of the slice: x: 2, y: 2, z: 4, core: 2. Of those that a mesh axis runs over, the one named last changes fastest.
Arguments:
- entering: bfloat16 [2, 8, 8192], P('section', None, 'kvp'), may hold values from -6 to 6
- newcomer: bfloat16 [1, 8, 8192], P(None, None, 'kvp'), may hold values from -6 to 6
- norm_gain: bfloat16 [2, 8192], P('section'), may hold values from 0.25 to 1.75
- query_weight: bfloat16 [2, 8192, 8192], P('section', None, 'kvp'), may hold values from -0.0625 to 0.0625
- keyvalue_weight: bfloat16 [2, 8192, 2048], P('section', None, 'kvp'), may hold values from -0.0625 to 0.0625
- key_cache: bfloat16 [2, 2, 8, 512, 1024], P('section', None, None, 'kvp'), may hold values from -96 to 96
- value_cache: bfloat16 [2, 2, 8, 512, 1024], P('section', None, None, 'kvp'), may hold values from -6 to 6
- cache_lengths: int32 [3, 8], replicated, may hold values from 1 to 512, as said below
Outputs:
- layer_outputs: bfloat16 [2, 2, 8, 8192], P('section', None, None, 'kvp')
Inputs may be any that keep to these rules, and one draw needn't show every extreme that they name: `cache_lengths`: in every micro-batch some request has exactly 512 cached positions.
All inputs are finite; a program needn't handle non-finite values.
Results may differ from a plain program's by a relative error of at most 0.024.
The roundings to bfloat16 on the way count: a program that leaves them out, or rounds other values in their place, can miss the bound.
Values may be sent and summed in bfloat16 or wider, within the bound.
A program may use at most 128 MiB of HBM per device.

v0:
```python
import math

import jax
import jax.numpy as jnp
from jax import lax
from jax.sharding import PartitionSpec as P

NH = 64
KVH = 8
HD = 128
REQ = 8
TICKS = 2


def combined_all(value, axis, join):
    pieces = jax.tree.map(lambda part: lax.all_gather(part, axis), value)
    head = jax.tree.map(lambda part: part[0], pieces)
    tail = jax.tree.map(lambda part: part[1:], pieces)
    running, _ = lax.scan(lambda running, section: (join(running, section), None), head, tail)
    return running


def shifted(shard, axis, by):
    devices = lax.axis_size(axis)
    pairs = [(i, i + by) for i in range(devices) if 0 <= i + by < devices]
    return lax.ppermute(shard, axis, pairs)


def rotate(values, positions):
    half_width = values.shape[-1] // 2
    exponent = jnp.arange(half_width, dtype=jnp.float32) * (2.0 / values.shape[-1])
    frequency = jnp.power(jnp.float32(500000.0), -exponent)
    angles = positions.astype(jnp.float32)[:, None, None] * frequency
    cosine = jnp.cos(angles)
    sine = jnp.sin(angles)
    first = values[..., :half_width]
    second = values[..., half_width:]
    return jnp.concatenate(
        [first * cosine - second * sine, second * cosine + first * sine], axis=-1
    )


def combine_parts(earlier, later):
    max_first, sum_first, out_first = earlier
    max_second, sum_second, out_second = later
    joined_max = jnp.maximum(max_first, max_second)
    factor_first = jnp.exp(max_first - joined_max)
    factor_second = jnp.exp(max_second - joined_max)
    joined_sum = sum_first * factor_first + sum_second * factor_second
    joined_out = out_first * factor_first[..., None] + out_second * factor_second[..., None]
    return (joined_max, joined_sum, joined_out)


def shards(
    entering,
    newcomer,
    norm_gain,
    query_weight,
    keyvalue_weight,
    key_cache,
    value_cache,
    cache_lengths,
):
    kvp_count = lax.axis_size("kvp")
    section_count = lax.axis_size("section")
    kvp_index = lax.axis_index("kvp")
    section_index = lax.axis_index("section")
    local_width = entering.shape[2]
    heads_local = NH // kvp_count
    local_positions = key_cache.shape[3]
    group_size = NH // KVH
    score_scale = 1.0 / math.sqrt(HD)
    gain_float = norm_gain[0].astype(jnp.float32)
    positions = kvp_index * local_positions + jnp.arange(local_positions, dtype=jnp.int32)
    outputs = []
    previous = entering[0]
    for tick in range(TICKS):
        if tick == 0:
            own_input = entering[0]
        else:
            received = shifted(previous, "section", 1)
            own_input = jnp.where(section_index == 0, newcomer[tick - 1], received)
        micro_id = tick + section_count - 1 - section_index
        lengths_now = lax.dynamic_index_in_dim(cache_lengths, micro_id, 0, keepdims=False)
        full_input = lax.all_gather(own_input, "kvp", axis=1, tiled=True)
        x_float = full_input.astype(jnp.float32)
        mean_square = jnp.mean(x_float * x_float, axis=-1, keepdims=True)
        normed = (x_float * lax.rsqrt(mean_square + 1e-05) * gain_float).astype(jnp.bfloat16)
        query_local = jnp.dot(normed, query_weight[0], preferred_element_type=jnp.float32)
        query_local = rotate(query_local.reshape(REQ, heads_local, HD), lengths_now)
        query_local = query_local.astype(jnp.bfloat16).reshape(REQ, heads_local * HD)
        fresh_local = jnp.dot(
            normed, keyvalue_weight[0], preferred_element_type=jnp.float32
        ).astype(jnp.bfloat16)
        query_all = lax.all_gather(query_local, "kvp", axis=1, tiled=True)
        fresh_all = lax.all_gather(fresh_local, "kvp", axis=1, tiled=True)
        grouped = query_all.reshape(REQ, KVH, group_size, HD)
        new_key = rotate(
            fresh_all[:, : KVH * HD].reshape(REQ, KVH, HD).astype(jnp.float32), lengths_now
        )
        new_value = fresh_all[:, KVH * HD :].reshape(REQ, KVH, HD).astype(jnp.float32)
        cached_keys = key_cache[0, tick].reshape(REQ, local_positions, KVH, HD)
        cached_values = value_cache[0, tick].reshape(REQ, local_positions, KVH, HD)
        scores = (
            jnp.einsum("bgrd,bpgd->bgrp", grouped, cached_keys, preferred_element_type=jnp.float32)
            * score_scale
        )
        in_cache = (positions[None, :] < lengths_now[:, None])[:, None, None, :]
        scores = jnp.where(in_cache, scores, jnp.float32(-1e30))
        part_max = jnp.max(scores, axis=-1)
        weights = jnp.where(in_cache, jnp.exp(scores - part_max[..., None]), jnp.float32(0.0))
        part_sum = jnp.sum(weights, axis=-1)
        value_weights = weights.astype(jnp.bfloat16)
        part_out = jnp.einsum(
            "bgrp,bpgd->bgrd", value_weights, cached_values, preferred_element_type=jnp.float32
        )
        new_score = jnp.einsum("bgrd,bgd->bgr", grouped.astype(jnp.float32), new_key) * score_scale
        whole_max, whole_sum, whole_out = combined_all(
            (part_max, part_sum, part_out), "kvp", combine_parts
        )
        top_score = jnp.maximum(whole_max, new_score)
        old_factor = jnp.exp(whole_max - top_score)
        new_weight = jnp.exp(new_score - top_score)
        denominator = whole_sum * old_factor + new_weight
        numerator = (
            whole_out * old_factor[..., None] + new_weight[..., None] * new_value[:, :, None, :]
        )
        attended = (numerator / denominator[..., None]).reshape(REQ, NH * HD)
        own_attended = lax.dynamic_slice_in_dim(attended, kvp_index * local_width, local_width, 1)
        previous = (own_input.astype(jnp.float32) + own_attended).astype(jnp.bfloat16)
        outputs.append(previous)
    return jnp.stack(outputs, axis=0)[None]


def solution(mesh):
    placed = (
        P("section", None, "kvp"),
        P(None, None, "kvp"),
        P("section", None),
        P("section", None, "kvp"),
        P("section", None, "kvp"),
        P("section", None, None, "kvp", None),
        P("section", None, None, "kvp", None),
        P(),
    )
    return jax.shard_map(
        shards,
        mesh=mesh,
        in_specs=placed,
        out_specs=P("section", None, None, "kvp"),
        check_vma=False,
    )
```

profile of v0, /device:TPU:3, one launch (start us, length us, event | category | flops | bytes accessed | tf_op | source)
XLA Modules:
  0.0 320.7 jit_solution(7186508386446411965)
XLA Ops:
  7.5 22.8 %all-gather = bf16[1,8,8192]{2,1,0:T(8,128)(2,1)S(1)} all-gather(bf16[1,8,512]{2,1,0:T(8,128)(2,1)} %param.12), channel_id=2, replica_groups=mesh['section'=2,'kvp'=16] {'kvp'}, dimensions={2}, use_global_device_ids=true | all-gather | bytes 139264 | tf_op jit(solution)/shard_map/all_gather | solution.py:85
  30.5 2.1 fusion.87
  33.7 11.5 %copy.33 = bf16[512,8192]{1,0:T(8,128)(2,1)} copy(bf16[512,8192]{0,1:T(8,128)(2,1)} %bitcast.174) | data formatting | bytes 16777216 | tf_op jit(solution)/shard_map/dot_general | solution.py:89
  45.4 5.6 %fusion.44 = f32[8,4,128]{2,0,1:T(8,128)S(1)} fusion(bf16[4,128,8192]{2,1,0:T(8,128)(2,1)} %bitcast.172, bf16[1,8,8192]{2,1,0:T(8,128)(2,1)S(1)} %all-gather, f32[8192]{0:T(1024)S(1)} %bitcast.189, f32[8]{0:T(128)S(1)} %add_rsqrt_fusion.1), kind=kOutput, calls=%fused_computation.60 | convolution fusion | flops 67371008 | bytes 8568864 | tf_op jit(solution)/shard_map/dot_general | solution.py:89
  51.2 17.8 %all_gather.55 = bf16[8,8192]{1,0:T(8,128)(2,1)S(1)} all-gather(bf16[8,512]{1,0:T(8,128)(2,1)S(1)} %maximum_bitcast_fusion.3), channel_id=1, replica_groups=mesh['section'=2,'kvp'=16] {'kvp'}, dimensions={1}, use_global_device_ids=true | all-gather | bytes 139264 | tf_op jit(solution)/shard_map/all_gather | solution.py:95
  71.8 22.0 %all-gather.1 = f32[128,8,8]{2,1,0:T(8,128)S(1)} all-gather(f32[8,8,8]{2,1,0:T(8,128)} %copy-done.6), channel_id=3, replica_groups=mesh['section'=2,'kvp'=16] {'kvp'}, dimensions={0}, use_global_device_ids=true | all-gather | bytes 34816 | tf_op jit(solution)/shard_map/all_gather | solution.py:16
  95.7 20.3 %all-gather.2 = f32[128,8,8]{2,1,0:T(8,128)S(1)} all-gather(f32[8,8,8]{2,1,0:T(8,128)S(1)} %fusion.31), channel_id=4, replica_groups=mesh['section'=2,'kvp'=16] {'kvp'}, dimensions={0}, use_global_device_ids=true | all-gather | bytes 34816 | tf_op jit(solution)/shard_map/all_gather | solution.py:16
  117.2 19.8 %all_gather.62 = bf16[8,2048]{1,0:T(8,128)(2,1)S(1)} all-gather(bf16[8,128]{1,0:T(8,128)(2,1)S(1)} %fusion.12), channel_id=1, replica_groups=mesh['section'=2,'kvp'=16] {'kvp'}, dimensions={1}, use_global_device_ids=true | all-gather | bytes 34816 | tf_op jit(solution)/shard_map/all_gather | solution.py:96
  138.0 4.6 %slice.131 = f32[120,8,8,128]{3,2,1,0:T(8,128)} slice(f32[128,8,8,128]{3,2,1,0:T(8,128)} %all-gather.10.cloned.1.call-done), slice={[8:128], [0:8], [0:8], [0:128]} | slice | bytes 7864320 | tf_op jit(solution)/shard_map/slice | solution.py:18
  142.6 30.8 %while.28 = (s32[]{:T(128)}, f32[8,8,8]{2,1,0:T(8,128)S(1)}, f32[8,8,8]{2,1,0:T(8,128)S(1)}, f32[8,8,8,128]{3,2,1,0:T(8,128)S(1)}, f32[15,8,8,8]{3,2,1,0:T(8,128...) while((s32[]{:T(128)}, f32[8,8,8]{2,1,0:T(8,128)S(1)}, ...), condition=%wide.region_4.5_spmd, body=%wide.region_3.4_spmd.sunk | while | flops 199682 | bytes 807013 | solution.py:19
  143.5 1.2 fusion.97
  147.6 1.2 fusion.97
  149.6 1.2 fusion.97
  153.7 1.2 fusion.97
  155.8 1.2 fusion.97
  159.9 1.2 fusion.97
  166.0 1.2 fusion.97
  170.1 1.2 fusion.97
  172.2 1.2 fusion.97
  174.7 1.3 collective-permute-start
  176.2 2.9 collective-permute-done
  179.8 18.6 %all_gather.63 = bf16[8,8192]{1,0:T(8,128)(2,1)S(1)} all-gather(bf16[8,512]{1,0:T(8,128)(2,1)S(1)} %bitcast_select_fusion), channel_id=1, replica_groups=mesh['section'=2,'kvp'=16] {'kvp'}, dimensions={1}, use_global_device_ids=true | all-gather | bytes 139264 | tf_op jit(solution)/shard_map/all_gather | solution.py:85
  198.6 5.6 %fusion.42 = f32[8,4,128]{2,0,1:T(8,128)S(1)} fusion(bf16[4,128,8192]{2,1,0:T(8,128)(2,1)} %bitcast.173, bf16[8,8192]{1,0:T(8,128)(2,1)S(1)} %all_gather.63, f32[8]{0:T(128)S(1)} %add_rsqrt_fusion, f32[8192]{0:T(1024)S(1)} %bitcast.192), kind=kOutput, calls=%fused_computation.58 | convolution fusion | flops 67371008 | bytes 8568864 | tf_op jit(solution)/shard_map/dot_general | solution.py:89
  204.4 19.4 %all_gather.64 = bf16[8,8192]{1,0:T(8,128)(2,1)S(1)} all-gather(bf16[8,512]{1,0:T(8,128)(2,1)S(1)} %maximum_bitcast_fusion.4), channel_id=1, replica_groups=mesh['section'=2,'kvp'=16] {'kvp'}, dimensions={1}, use_global_device_ids=true | all-gather | bytes 139264 | tf_op jit(solution)/shard_map/all_gather | solution.py:95
  225.5 20.3 %all-gather.4 = f32[128,8,8]{2,1,0:T(8,128)S(1)} all-gather(f32[8,8,8]{2,1,0:T(8,128)S(1)} %get-tuple-element.163), channel_id=6, replica_groups=mesh['section'=2,'kvp'=16] {'kvp'}, dimensions={0}, use_global_device_ids=true | all-gather | bytes 34816 | tf_op jit(solution)/shard_map/all_gather | solution.py:16
  246.1 21.8 %all-gather.5 = f32[128,8,8]{2,1,0:T(8,128)S(1)} all-gather(f32[8,8,8]{2,1,0:T(8,128)S(1)} %fusion.33), channel_id=7, replica_groups=mesh['section'=2,'kvp'=16] {'kvp'}, dimensions={0}, use_global_device_ids=true | all-gather | bytes 34816 | tf_op jit(solution)/shard_map/all_gather | solution.py:16
  269.2 18.2 %all_gather.71 = bf16[8,2048]{1,0:T(8,128)(2,1)S(1)} all-gather(bf16[8,128]{1,0:T(8,128)(2,1)S(1)} %fusion.15), channel_id=1, replica_groups=mesh['section'=2,'kvp'=16] {'kvp'}, dimensions={1}, use_global_device_ids=true | all-gather | bytes 34816 | tf_op jit(solution)/shard_map/all_gather | solution.py:96
  288.4 4.6 %slice.143 = f32[120,8,8,128]{3,2,1,0:T(8,128)} slice(f32[128,8,8,128]{3,2,1,0:T(8,128)} %all-gather.12.cloned.1.call-done), slice={[8:128], [0:8], [0:8], [0:128]} | slice | bytes 7864320 | tf_op jit(solution)/shard_map/slice | solution.py:18
  293.0 19.1 %while.29 = (s32[]{:T(128)}, f32[8,8,8]{2,1,0:T(8,128)S(1)}, f32[8,8,8]{2,1,0:T(8,128)S(1)}, f32[8,8,8,128]{3,2,1,0:T(8,128)S(1)}, f32[15,8,8,8]{3,2,1,0:T(8,128...) while((s32[]{:T(128)}, f32[8,8,8]{2,1,0:T(8,128)S(1)}, ...), condition=%wide.region_9.10_spmd, body=%wide.region_8.9_spmd.sunk | while | flops 199682 | bytes 807013 | solution.py:19
  295.6 1.2 fusion.99
  296.8 1.2 fusion.99
  298.1 1.2 fusion.99
  (153 shorter events, 52.7 us)
Async XLA Ops:
  6.5 110.3 %copy-start = (bf16[1,8192,128]{2,1,0:T(8,128)(2,1)S(1)}, bf16[1,8192,128]{2,1,0:T(8,128)(2,1)}, u32[]{:S(2)}) copy-start(bf16[1,8192,128]{2,1,0:T(8,128)(2,1)} %param.16) | copy-start | bytes 6291460
  6.5 131.5 %all-gather.10.cloned.1.call-start = ((), (), s32[]{:S(2)}) async-start(), calls=%async_computation | async-start | bytes 4456448 | tf_op jit(solution)/shard_map/all_gather | solution.py:16
  6.6 26.1 %copy-start.3 = (bf16[1,2,8,32,1024]{4,3,2,1,0:T(8,128)(2,1)S(1)}, bf16[1,2,8,32,1024]{4,3,2,1,0:T(8,128)(2,1)}, u32[]{:S(2)}) copy-start(bf16[1,2,8,32,1024]{4,3,2,1,0:T(8,128)(2,1)} %param.18) | copy-start | bytes 3145732
  7.5 37.8 %copy-start.4 = (f32[1,8192]{1,0:T(1,128)}, f32[1,8192]{1,0:T(1,128)S(1)}, u32[]{:S(2)}) copy-start(f32[1,8192]{1,0:T(1,128)S(1)} %mul.391) | copy-start | bytes 98308
  30.5 14.9 %copy-start.16 = (f32[8]{0:T(128)}, f32[8]{0:T(128)S(1)}, u32[]{:S(2)}) copy-start(f32[8]{0:T(128)S(1)} %add_rsqrt_fusion.1) | copy-start | bytes 100
  33.7 11.5 %copy-start.19 = (s32[3,8]{1,0:T(4,128)S(1)}, s32[3,8]{1,0:T(4,128)}, u32[]{:S(2)}) copy-start(s32[3,8]{1,0:T(4,128)} %param.19) | copy-start | bytes 292
  69.0 1.0 copy-start.7
  69.6 0.6 copy-start.15
  70.0 0.6 copy-start.6
  70.0 46.8 %copy-start.5 = (f32[1,8192]{1,0:T(1,128)S(1)}, f32[1,8192]{1,0:T(1,128)}, u32[]{:S(2)}) copy-start(f32[1,8192]{1,0:T(1,128)} %copy-done.4) | copy-start | bytes 98308
  70.0 46.8 %copy-start.17 = (f32[8]{0:T(128)S(1)}, f32[8]{0:T(128)}, u32[]{:S(2)}) copy-start(f32[8]{0:T(128)} %copy-done.16) | copy-start | bytes 100
  70.0 67.1 %copy-start.8 = (bf16[8,8192]{1,0:T(8,128)(2,1)S(1)}, bf16[8,8192]{1,0:T(8,128)(2,1)}, u32[]{:S(2)}) copy-start(bf16[8,8192]{1,0:T(8,128)(2,1)} %copy-done.7) | copy-start | bytes 393220
  71.7 216.7 %all-gather.12.cloned.1.call-start = ((), (), s32[]{:S(2)}) async-start(), calls=%async_computation.1 | async-start | bytes 4456448 | tf_op jit(solution)/shard_map/all_gather | solution.py:16
  138.0 4.6 %slice-start = ((f32[128,8,8,128]{3,2,1,0:T(8,128)}), f32[8,8,8,128]{3,2,1,0:T(8,128)S(1)}, s32[]{:S(2)}) async-start(f32[128,8,8,128]{3,2,1,0:T(8,128)} %all-gather.10.cloned.1.call-done), calls=%async_computation.2 | async-start | bytes 524288 | tf_op jit(solution)/shard_map/slice | solution.py:17
  142.6 32.1 %copy-start.11 = (bf16[1,8,512]{2,1,0:T(8,128)(2,1)S(1)}, bf16[1,8,512]{2,1,0:T(8,128)(2,1)}, u32[]{:S(2)}) copy-start(bf16[1,8,512]{2,1,0:T(8,128)(2,1)} %param.12) | copy-start | bytes 24580
  142.6 33.4 %copy-start.1 = (bf16[1,1,8,32,1024]{4,3,2,1,0:T(8,128)(2,1)S(1)}, bf16[1,1,8,32,1024]{4,3,2,1,0:T(8,128)(2,1)}, u32[]{:S(2)}) copy-start(bf16[1,1,8,32,1024]{4,3,2,1,0:T(8,128)(2,1)} %get-tuple-element.138) | copy-start | bytes 1572868
  142.6 33.5 %copy-start.2 = (bf16[1,1,8,32,1024]{4,3,2,1,0:T(8,128)(2,1)S(1)}, bf16[1,1,8,32,1024]{4,3,2,1,0:T(8,128)(2,1)}, u32[]{:S(2)}) copy-start(bf16[1,1,8,32,1024]{4,3,2,1,0:T(8,128)(2,1)} %get-tuple-element.135) | copy-start | bytes 1572868
  174.6 29.6 %copy-start.12 = (bf16[8,512]{1,0:T(8,128)(2,1)}, bf16[8,512]{1,0:T(8,128)(2,1)S(1)}, u32[]{:S(2)}) copy-start(bf16[8,512]{1,0:T(8,128)(2,1)S(1)} %fusion.70) | copy-start | bytes 24580
  174.7 4.4 %collective-permute-start = (bf16[8,512]{1,0:T(8,128)(2,1)S(1)}, bf16[8,512]{1,0:T(8,128)(2,1)S(1)}, u32[]{:S(2)}, u32[]{:S(2)}) collective-permute-start(bf16[8,512]{1,0:T(8,128)(2,1)S(1)} %fusion.70), channel_id=1, source_target_pairs={{0,16},{1,17},{2,18},{3,19},{4,20},{5,21},{6,22},{7,23},{8,24},{9,... | collective-permute-start | bytes 24584 | tf_op jit(solution)/shard_map/ppermute | solution.py:26
  198.6 5.7 %copy-start.18 = (f32[8]{0:T(128)}, f32[8]{0:T(128)S(1)}, u32[]{:S(2)}) copy-start(f32[8]{0:T(128)S(1)} %add_rsqrt_fusion) | copy-start | bytes 100
  198.6 25.2 %copy-start.14 = (pred[8,32]{1,0:T(8,128)(4,1)S(1)}, pred[8,32]{1,0:T(8,128)(4,1)}, u32[]{:S(2)}) copy-start(pred[8,32]{1,0:T(8,128)(4,1)} %get-tuple-element.160) | copy-start | bytes 772
  223.8 0.6 copy-start.9
  225.5 62.0 %copy-start.10 = (bf16[8,8192]{1,0:T(8,128)(2,1)S(1)}, bf16[8,8192]{1,0:T(8,128)(2,1)}, u32[]{:S(2)}) copy-start(bf16[8,8192]{1,0:T(8,128)(2,1)} %copy-done.9) | copy-start | bytes 393220
  288.4 4.6 %slice-start.1 = ((f32[128,8,8,128]{3,2,1,0:T(8,128)}), f32[8,8,8,128]{3,2,1,0:T(8,128)S(1)}, s32[]{:S(2)}) async-start(f32[128,8,8,128]{3,2,1,0:T(8,128)} %all-gather.12.cloned.1.call-done), calls=%async_computation.3 | async-start | bytes 524288 | tf_op jit(solution)/shard_map/slice | solution.py:17
  293.0 20.3 %copy-start.13 = (bf16[8,512]{1,0:T(8,128)(2,1)S(1)}, bf16[8,512]{1,0:T(8,128)(2,1)}, u32[]{:S(2)}) copy-start(bf16[8,512]{1,0:T(8,128)(2,1)} %copy-done.12) | copy-start | bytes 24580
Sparse Core Ops, SparseCore 0:
  71.8 53.3 all-gather.9
  225.6 52.5 all-gather.11
where the time goes:
time: 324 us; the launch traced here: 321 us
  blocking collectives  201 us (62%)
  other arithmetic  56.7 us (18%)
  local copies, waits for them, and re-layouts  27 us (8%)
  matrix products  17.5 us (5%)
  between operations  13.7 us (4%)
    all_gather x4, blocking collectives, combined_all(): pieces = jax.tree.map(lambda part: lax.all_gather(part, axis), value)  84.4 us
    all_gather x2, blocking collectives, shards(): full_input = lax.all_gather(own_input, 'kvp', axis=1, tiled=True)  41.4 us
    all_gather x2, blocking collectives, shards(): fresh_all = lax.all_gather(fresh_local, 'kvp', axis=1, tiled=True)  38 us
    all_gather x2, blocking collectives, shards(): query_all = lax.all_gather(query_local, 'kvp', axis=1, tiled=True)  37.2 us
    add x30, other arithmetic, combine_parts(): out_first * factor_first[..., None] + out_second * factor_second[..., None]  36.4 us
    add x30, other arithmetic, combine_parts(): joined_sum = sum_first * factor_first + sum_second * factor_second  12.8 us
    dot_general x1, local copies, waits for them, and re-layouts, shards(): jnp.dot(normed, query_weight[0], preferred_element_type=jnp.float32)  11.5 us
    dot_general x2, matrix products, shards(): jnp.dot(normed, query_weight[0], preferred_element_type=jnp.float32)  11.3 us
  transfers between devices with their start and end apart: 3, of which 1 were waited for; matrix products, arithmetic and copies ran while one was open for 2% of the time, Pallas kernels for 0%

commit v1 on v0

v1 whole, which is shorter than its diff:
```python
import functools
import math

import jax
import jax.numpy as jnp
from jax import lax
from jax.experimental import pallas as pl
from jax.experimental.pallas import tpu as pltpu
from jax.sharding import PartitionSpec as P

NH = 64
KVH = 8
HD = 128
GROUP = NH // KVH
THETA = 500000.0
EPS = 1e-05
NEG = -1e30
MESH = pl.DeviceIdType.MESH
F32 = jnp.float32
BF16 = jnp.bfloat16


def three_parts(row):
    high = row.astype(BF16).astype(F32)
    rest = row - high
    middle = rest.astype(BF16).astype(F32)
    return [high, middle, rest - middle]


def layer_kernel(
    n,
    sections,
    lengths_ref,
    entering_ref,
    newcomer_ref,
    gain_hbm,
    query_hbm,
    keyvalue_hbm,
    keys_hbm,
    values_hbm,
    out_ref,
    query_w,
    keyvalue_w,
    keys,
    values,
    gain,
    inputs,
    normed,
    heads,
    staged,
    parts,
    leaving,
    columns,
    load_sem,
    weight_sem,
    cache_sem,
    send_sem,
    recv_sem,
):
    ticks, rows, width = out_ref.shape
    features = query_w.shape[0]
    own_heads = NH // n
    own_rows = own_heads * rows
    kv_width = keyvalue_w.shape[1]
    pieces = HD // kv_width
    group_rows = GROUP * rows
    span = keys.shape[1] // rows
    chunks = weight_sem.shape[0]
    depth = features // chunks
    scale = 1.0 / math.sqrt(HD)

    section = lax.axis_index("section")
    me = lax.axis_index("kvp")

    gain_load = pltpu.make_async_copy(gain_hbm, gain, load_sem.at[0])
    gain_load.start()
    own_loads = [
        pltpu.make_async_copy(entering_ref, inputs.at[0, me], load_sem.at[1])
    ]
    own_loads[0].start()
    weight_loads = []
    for c in range(chunks):
        part = pl.ds(c * depth, depth)
        weight_loads.append(
            (
                pltpu.make_async_copy(query_hbm.at[part], query_w.at[part], weight_sem.at[c, 0]),
                pltpu.make_async_copy(
                    keyvalue_hbm.at[part], keyvalue_w.at[part], weight_sem.at[c, 1]
                ),
            )
        )
        for load in weight_loads[-1]:
            load.start()
    cache_loads = []
    for t in range(ticks):
        cache_loads.append(
            (
                pltpu.make_async_copy(keys_hbm.at[t], keys.at[t], cache_sem.at[t, 0]),
                pltpu.make_async_copy(values_hbm.at[t], values.at[t], cache_sem.at[t, 1]),
            )
        )
        for load in cache_loads[-1]:
            load.start()

    def peer(step):
        return lax.rem(me + step, n)

    barrier = pltpu.get_barrier_semaphore()

    def greet(step, carry):
        pl.semaphore_signal(
            barrier, inc=1, device_id=(section, peer(step)), device_id_type=MESH
        )
        return carry

    lax.fori_loop(1, n, greet, 0)
    if sections > 1:

        @pl.when(section < sections - 1)
        def _():
            def greet_next(step, carry):
                pl.semaphore_signal(
                    barrier, inc=1, device_id=(section + 1, peer(step)), device_id_type=MESH
                )
                return carry

            lax.fori_loop(0, n, greet_next, 0)

        @pl.when(section > 0)
        def _():
            def greet_previous(step, carry):
                pl.semaphore_signal(
                    barrier, inc=1, device_id=(section - 1, peer(step)), device_id_type=MESH
                )
                return carry

            lax.fori_loop(0, n, greet_previous, 0)

    neighbours = (section > 0).astype(jnp.int32) + (section < sections - 1).astype(jnp.int32)
    pl.semaphore_wait(barrier, n - 1 + n * neighbours)

    def spread(source, target, tick, phase):
        def send(step, carry):
            pltpu.make_async_remote_copy(
                src_ref=source,
                dst_ref=target,
                send_sem=send_sem.at[tick, phase],
                recv_sem=recv_sem.at[tick, phase],
                device_id=(section, peer(step)),
                device_id_type=MESH,
            ).start()
            return carry

        lax.fori_loop(1, n, send, 0)

    def arrived(buffer, count, sem):
        whole = buffer.at[pl.ds(0, count)]
        pltpu.make_async_copy(whole, whole, sem).wait()

    spread(entering_ref, inputs.at[0, me], 0, 0)

    @pl.when(section == 0)
    def _():
        for t in range(1, ticks):
            pltpu.make_async_copy(
                newcomer_ref.at[t - 1], inputs.at[t, me], load_sem.at[1 + t]
            ).start()
            spread(newcomer_ref.at[t - 1], inputs.at[t, me], t, 0)

    lane = lax.broadcasted_iota(jnp.int32, (rows, HD), 1)
    row = lax.broadcasted_iota(jnp.int32, (rows, HD), 0)
    half = HD // 2
    exponent = (lane % half).astype(F32) * (2.0 / HD)
    frequency = jnp.exp(exponent * (-math.log(THETA)))
    turns = []
    masks = []
    place = lax.broadcasted_iota(jnp.int32, (rows * span, group_rows), 0)
    column = lax.broadcasted_iota(jnp.int32, (rows * span, group_rows), 1)
    position = me * span + place % span
    for t in range(ticks):
        micro = t + sections - 1 - section
        by_row = jnp.zeros((rows, HD), jnp.int32)
        limit = jnp.zeros((rows * span, group_rows), jnp.int32)
        for b in range(rows):
            length = lengths_ref[micro, b]
            by_row = jnp.where(row == b, length, by_row)
            limit = jnp.where(column % rows == b, length, limit)
        angles = by_row.astype(F32) * frequency
        sine = jnp.sin(angles)
        turns.append((jnp.cos(angles), jnp.where(lane < half, -sine, sine)))
        masks.append((place // span == column % rows) & (position < limit))

    def rotated(head, t):
        cosine, sine = turns[t]
        return head * cosine + pltpu.roll(head, half, 1) * sine

    gain_load.wait()
    for t in range(ticks):
        if t == 0:
            own_loads[0].wait()
            arrived(inputs.at[0], n - 1, recv_sem.at[0, 0])
        else:

            @pl.when(section == 0)
            def _():
                pltpu.make_async_copy(
                    newcomer_ref.at[t - 1], inputs.at[t, me], load_sem.at[1 + t]
                ).wait()
                arrived(inputs.at[t], n - 1, recv_sem.at[t, 0])

            @pl.when(section > 0)
            def _():
                arrived(inputs.at[t], n, recv_sem.at[t, 0])

        squares = jnp.zeros((rows, width), F32)
        for s in range(n):
            x = inputs[t, s].astype(F32)
            squares = squares + x * x
        mean_square = jnp.sum(squares, axis=-1, keepdims=True) * (1.0 / features)
        factor = lax.rsqrt(mean_square + EPS)
        for s in range(n):
            part = pl.ds(s * width, width)
            x = inputs[t, s].astype(F32)
            normed[:, part] = (x * factor * gain[:, part].astype(F32)).astype(BF16)

        query = jnp.zeros((rows, width), F32)
        fresh = jnp.zeros((rows, kv_width), F32)
        for c in range(chunks):
            part = pl.ds(c * depth, depth)
            if t == 0:
                for load in weight_loads[c]:
                    load.wait()
            query = query + jnp.dot(normed[:, part], query_w[part], preferred_element_type=F32)
            fresh = fresh + jnp.dot(normed[:, part], keyvalue_w[part], preferred_element_type=F32)
        message = [
            rotated(query[:, h * HD : (h + 1) * HD], t) for h in range(own_heads)
        ]
        fresh = fresh.astype(BF16).astype(F32)
        if pieces > 1:
            fresh = jnp.concatenate([fresh] * pieces, axis=1)
            fresh = jnp.where(lane // kv_width == me % pieces, fresh, 0.0)
        message.append(fresh)
        spare = heads.shape[2] - own_rows - rows
        if spare:
            message.append(jnp.zeros((spare, HD), F32))
        heads[t, me] = jnp.concatenate(message, axis=0).astype(BF16)
        spread(heads.at[t, me], heads.at[t, me], t, 1)

        for load in cache_loads[t]:
            load.wait()
        arrived(heads.at[t], n - 1, recv_sem.at[t, 1])
        valid = masks[t]
        per_group = GROUP // own_heads
        for g in range(KVH):
            grouped = jnp.concatenate(
                [
                    heads[t, g * per_group + j].astype(F32)[:own_rows]
                    for j in range(per_group)
                ],
                axis=0,
            ).astype(BF16)
            part = pl.ds(g * HD, HD)
            scores = lax.dot_general(
                keys[t, :, part],
                grouped,
                (((1,), (1,)), ((), ())),
                preferred_element_type=F32,
            )
            scores = jnp.where(valid, scores * scale, NEG)
            top = jnp.max(scores, axis=0, keepdims=True)
            weights = jnp.where(valid, jnp.exp(scores - top), 0.0)
            total = jnp.sum(weights, axis=0, keepdims=True)
            weighted = lax.dot_general(
                weights.astype(BF16),
                values[t, :, part],
                (((0,), (0,)), ((), ())),
                preferred_element_type=F32,
            )
            stats = jnp.concatenate(
                three_parts(top) + three_parts(total) + [jnp.zeros((2, group_rows), F32)], axis=0
            )
            stats = jnp.concatenate([stats, jnp.zeros((8, HD - group_rows), F32)], axis=1)
            for j in range(per_group):
                target = g * per_group + j
                message = [weighted[j * own_rows : (j + 1) * own_rows], stats]
                if spare:
                    message.append(jnp.zeros((spare, HD), F32))
                message = jnp.concatenate(message, axis=0).astype(BF16)
                staged[t, target] = message

                @pl.when(target == me)
                def _():
                    parts[t, me] = message

                @pl.when(target != me)
                def _():
                    pltpu.make_async_remote_copy(
                        src_ref=staged.at[t, target],
                        dst_ref=parts.at[t, me],
                        send_sem=send_sem.at[t, 2],
                        recv_sem=recv_sem.at[t, 2],
                        device_id=(section, target),
                        device_id_type=MESH,
                    ).start()

        group = (me * own_heads) // GROUP
        new_key = jnp.zeros((rows, HD), F32)
        new_value = jnp.zeros((rows, HD), F32)
        for j in range(pieces):
            new_key = new_key + heads[t, group * pieces + j].astype(F32)[own_rows : own_rows + rows]
            new_value = (
                new_value
                + heads[t, n // 2 + group * pieces + j].astype(F32)[own_rows : own_rows + rows]
            )
        new_key = jnp.concatenate([rotated(new_key, t)] * own_heads, axis=0)
        new_value = jnp.concatenate([new_value] * own_heads, axis=0)
        own_query = heads[t, me].astype(F32)[:own_rows]
        new_score = jnp.sum(own_query * new_key, axis=-1, keepdims=True) * scale

        arrived(parts.at[t], n - 1, recv_sem.at[t, 2])
        tops = []
        totals = []
        for s in range(n):
            stats = parts[t, s].astype(F32)[own_rows : own_rows + 8]
            tops.append(stats[0:1] + stats[1:2] + stats[2:3])
            totals.append(stats[3:4] + stats[4:5] + stats[5:6])
        blank = HD - n
        tops = jnp.concatenate(tops + [jnp.full((blank, HD), NEG, F32)], axis=0)
        totals = jnp.concatenate(totals + [jnp.zeros((blank, HD), F32)], axis=0)
        columns[0] = tops.T
        columns[1] = totals.T
        first = pl.multiple_of((me % per_group) * own_rows, 8)
        tops = columns[0, pl.ds(first, own_rows), :]
        totals = columns[1, pl.ds(first, own_rows), :]
        top = jnp.maximum(jnp.max(tops, axis=-1, keepdims=True), new_score)
        factors = jnp.exp(tops - top)
        new_weight = jnp.exp(new_score - top)
        denominator = jnp.sum(factors * totals, axis=-1, keepdims=True) + new_weight
        numerator = new_weight * new_value
        for s in range(n):
            part = parts[t, s].astype(F32)[:own_rows]
            numerator = numerator + part * factors[:, s : s + 1]
        attended = numerator / denominator
        attended = jnp.concatenate(
            [attended[h * rows : (h + 1) * rows] for h in range(own_heads)], axis=1
        )
        result = (inputs[t, me].astype(F32) + attended).astype(BF16)
        out_ref[t] = result
        if t < ticks - 1 and sections > 1:
            leaving[t] = result

            @pl.when(section < sections - 1)
            def _():
                def send(step, carry):
                    pltpu.make_async_remote_copy(
                        src_ref=leaving.at[t],
                        dst_ref=inputs.at[t + 1, me],
                        send_sem=send_sem.at[t, 3],
                        recv_sem=recv_sem.at[t + 1, 0],
                        device_id=(section + 1, peer(step)),
                        device_id_type=MESH,
                    ).start()
                    return carry

                lax.fori_loop(0, n, send, 0)

    for t in range(ticks):
        if t == 0:
            arrived(inputs.at[t], n - 1, send_sem.at[t, 0])
        else:

            @pl.when(section == 0)
            def _():
                arrived(inputs.at[t], n - 1, send_sem.at[t, 0])

        arrived(heads.at[t], n - 1, send_sem.at[t, 1])
        arrived(parts.at[t], n - 1, send_sem.at[t, 2])
        if t < ticks - 1 and sections > 1:

            @pl.when(section < sections - 1)
            def _():
                arrived(inputs.at[t], n, send_sem.at[t, 3])


def shards(
    n,
    sections,
    entering,
    newcomer,
    norm_gain,
    query_weight,
    keyvalue_weight,
    key_cache,
    value_cache,
    cache_lengths,
):
    _, rows, width = entering.shape
    _, features, _ = query_weight.shape
    kv_width = keyvalue_weight.shape[2]
    _, ticks, _, span, kv_features = key_cache.shape
    own_rows = (NH // n) * rows
    message_rows = -(-(own_rows + 8) // 16) * 16
    chunks = 4
    anywhere = pl.BlockSpec(memory_space=pl.ANY)
    out = pl.pallas_call(
        functools.partial(layer_kernel, n, sections),
        out_shape=jax.ShapeDtypeStruct((ticks, rows, width), BF16),
        in_specs=[pl.BlockSpec(memory_space=pltpu.SMEM)] + [anywhere] * 7,
        out_specs=pl.BlockSpec(memory_space=pltpu.VMEM),
        scratch_shapes=[
            pltpu.VMEM((features, width), BF16),
            pltpu.VMEM((features, kv_width), BF16),
            pltpu.VMEM((ticks, rows * span, kv_features), BF16),
            pltpu.VMEM((ticks, rows * span, kv_features), BF16),
            pltpu.VMEM((1, features), BF16),
            pltpu.VMEM((ticks, n, rows, width), BF16),
            pltpu.VMEM((rows, features), BF16),
            pltpu.VMEM((ticks, n, message_rows, HD), BF16),
            pltpu.VMEM((ticks, n, message_rows, HD), BF16),
            pltpu.VMEM((ticks, n, message_rows, HD), BF16),
            pltpu.VMEM((ticks, rows, width), BF16),
            pltpu.VMEM((2, HD, HD), F32),
            pltpu.SemaphoreType.DMA((1 + ticks,)),
            pltpu.SemaphoreType.DMA((chunks, 2)),
            pltpu.SemaphoreType.DMA((ticks, 2)),
            pltpu.SemaphoreType.DMA((ticks, 4)),
            pltpu.SemaphoreType.DMA((ticks, 3)),
        ],
        compiler_params=pltpu.CompilerParams(
            collective_id=0, has_side_effects=True, vmem_limit_bytes=40 << 20
        ),
    )(
        cache_lengths,
        entering[0],
        newcomer,
        norm_gain,
        query_weight[0],
        keyvalue_weight[0],
        key_cache.reshape(ticks, rows * span, kv_features),
        value_cache.reshape(ticks, rows * span, kv_features),
    )
    return out[None]


def solution(mesh):
    placed = (
        P("section", None, "kvp"),
        P(None, None, "kvp"),
        P("section", None),
        P("section", None, "kvp"),
        P("section", None, "kvp"),
        P("section", None, None, "kvp", None),
        P("section", None, None, "kvp", None),
        P(),
    )
    return jax.shard_map(
        functools.partial(shards, mesh.shape["kvp"], mesh.shape["section"]),
        mesh=mesh,
        in_specs=placed,
        out_specs=P("section", None, None, "kvp"),
        check_vma=False,
    )
```

time: 324 us -> 60.8 us (0.19)
  blocking collectives: 201 us -> 0 us
  other arithmetic: 56.7 us -> 0 us
  Pallas kernels: 0 us -> 49 us
  matrix products: 17.5 us -> 0 us
  local copies, waits for them, and re-layouts: 27 us -> 10.9 us
  between operations: 13.7 us -> 0.02 us
    all_gather x10 -> x0, blocking collectives: 201 us -> none  [the longest x4 84.4 us: combined_all(): pieces = jax.tree.map(lambda part: lax.all_gather(part, axis), value)]
    add x63 -> x0, other arithmetic: 50.8 us -> none  [the longest x30 36.4 us: combine_parts(): out_first * factor_first[..., None] + out_second * factor_second[..., None]]
    pallas_call x0 -> x1, Pallas kernels: none -> 49 us  [shards(): pl.pallas_call(functools.partial(layer_kernel, n, sections), out_shape=ja...]
    dot_general x10 -> x0, matrix products: 17.5 us -> none  [the longest x2 11.3 us: shards(): jnp.dot(normed, query_weight[0], preferred_element_type=jnp.float32)]
    slice x16 -> x0, local copies, waits for them, and re-layouts: 13.9 us -> none  [the longest x6 10.9 us: combined_all(): tail = jax.tree.map(lambda part: part[1:], pieces)]
    dot_general x1 -> x0, local copies, waits for them, and re-layouts: 11.5 us -> none  [shards(): jnp.dot(normed, query_weight[0], preferred_element_type=jnp.float32)]
    unnamed x46 -> x17, local copies, waits for them, and re-layouts: 1.55 us -> 10.9 us
  transfers between devices with their start and end apart: 3 -> 0, of which waited for: 1 -> 0; matrix products, arithmetic and copies ran while one was open for 2% -> 0% of each run, Pallas kernels for 0% -> 0%
where the time goes in v1:
time: 60.8 us; the launch traced here: 59.9 us
  Pallas kernels  49 us (81%)
  local copies, waits for them, and re-layouts  10.9 us (18%)
    pallas_call x1, Pallas kernels, shards(): pl.pallas_call(functools.partial(layer_kernel, n, sections), out_shape=ja...  49 us
    unnamed x17, local copies, waits for them, and re-layouts  10.9 us

profile of v1, /device:TPU:3, one launch (start us, length us, event | category | flops | bytes accessed | tf_op | source)
XLA Modules:
  0.0 59.9 jit_solution(9542739087525257930)
XLA Ops:
  0.0 0.0 copy-start
  0.0 3.4 %copy-done = bf16[1,8192,512]{2,1,0:T(8,128)(2,1)S(1)} copy-done((bf16[1,8192,512]{2,1,0:T(8,128)(2,1)S(1)}, bf16[1,8192,512]{2,1,0:T(8,128)(2,1)}, u32[]{:S(2)}) %copy-start) | copy-done | bytes 8388632
  3.4 0.0 copy-start.1
  3.4 1.6 %copy-done.1 = bf16[1,8192,128]{2,1,0:T(8,128)(2,1)S(1)} copy-done((bf16[1,8192,128]{2,1,0:T(8,128)(2,1)S(1)}, bf16[1,8192,128]{2,1,0:T(8,128)(2,1)}, u32[]{:S(2)}) %copy-start.1) | copy-done | bytes 2097176
  5.0 0.0 copy-start.2
  5.0 1.2 %copy-done.2 = bf16[1,2,8,32,1024]{4,3,2,1,0:T(8,128)(2,1)S(1)} copy-done((bf16[1,2,8,32,1024]{4,3,2,1,0:T(8,128)(2,1)S(1)}, bf16[1,2,8,32,1024]{4,3,2,1,0:T(8,128)(2,1)}, u32[]{:S(2)}) %copy-start.2) | copy-done | bytes 1048600
  6.2 0.0 copy-start.3
  6.2 1.2 %copy-done.3 = bf16[1,2,8,32,1024]{4,3,2,1,0:T(8,128)(2,1)S(1)} copy-done((bf16[1,2,8,32,1024]{4,3,2,1,0:T(8,128)(2,1)S(1)}, bf16[1,2,8,32,1024]{4,3,2,1,0:T(8,128)(2,1)}, u32[]{:S(2)}) %copy-start.3) | copy-done | bytes 1048600
  7.4 0.0 copy-start.4
  7.4 0.8 %copy-done.4 = bf16[1,8192]{1,0:T(2,128)(2,1)S(1)} copy-done((bf16[1,8192]{1,0:T(2,128)(2,1)S(1)}, bf16[1,8192]{1,0:T(2,128)(2,1)}, u32[]{:S(2)}) %copy-start.4) | copy-done | bytes 16408
  8.2 0.0 copy-start.5
  8.2 0.7 %copy-done.5 = bf16[1,8,512]{2,1,0:T(8,128)(2,1)S(1)} copy-done((bf16[1,8,512]{2,1,0:T(8,128)(2,1)S(1)}, bf16[1,8,512]{2,1,0:T(8,128)(2,1)}, u32[]{:S(2)}) %copy-start.5) | copy-done | bytes 8216
  8.9 0.0 copy-start.6
  8.9 0.7 %copy-done.6 = bf16[1,8,512]{2,1,0:T(8,128)(2,1)S(1)} copy-done((bf16[1,8,512]{2,1,0:T(8,128)(2,1)S(1)}, bf16[1,8,512]{2,1,0:T(8,128)(2,1)}, u32[]{:S(2)}) %copy-start.6) | copy-done | bytes 8216
  9.6 0.0 copy-start.7
  9.6 0.7 %copy-done.7 = s32[3,8]{1,0:T(4,128)S(1)} copy-done((s32[3,8]{1,0:T(4,128)S(1)}, s32[3,8]{1,0:T(4,128)}, u32[]{:S(2)}) %copy-start.7) | copy-done | bytes 120
  10.3 49.0 %shard_map.82 = bf16[2,8,512]{2,1,0:T(8,128)(2,1)S(1)} custom-call(s32[3,8]{1,0:T(4,128)S(1)} %copy-done.7, bf16[8,512]{1,0:T(8,128)(2,1)S(1)} %bitcast.11, bf16[1,8,512]{2,1,0:T(8,128)(2,1)S(1)} %copy-done.6, bf16[1,8192]{1,0:T(2,128)(2,1)S(1)} %copy-done.4, bf16[8192,512]{1,0:T(8,128)(2,1)S(1)} %bitcast.6, bf16[8192,128]{1,0:T(8,128)(2,1)S(1)} %bitcast.7, ...), custom_call_target="tpu_custom_call" | custom-call | tf_op jit(solution)/shard_map/pallas_call | solution.py:405
  59.3 0.6 %copy.10 = bf16[1,2,8,512]{3,2,1,0:T(8,128)(2,1)} copy(bf16[1,2,8,512]{3,2,1,0:T(8,128)(2,1)S(1)} %bitcast.10) | data formatting | bytes 32768
Async XLA Ops:
  0.0 3.4 %copy-start = (bf16[1,8192,512]{2,1,0:T(8,128)(2,1)S(1)}, bf16[1,8192,512]{2,1,0:T(8,128)(2,1)}, u32[]{:S(2)}) copy-start(bf16[1,8192,512]{2,1,0:T(8,128)(2,1)} %param.11) | copy-start | bytes 25165828
  3.4 1.6 %copy-start.1 = (bf16[1,8192,128]{2,1,0:T(8,128)(2,1)S(1)}, bf16[1,8192,128]{2,1,0:T(8,128)(2,1)}, u32[]{:S(2)}) copy-start(bf16[1,8192,128]{2,1,0:T(8,128)(2,1)} %param.12) | copy-start | bytes 6291460
  5.0 1.2 %copy-start.2 = (bf16[1,2,8,32,1024]{4,3,2,1,0:T(8,128)(2,1)S(1)}, bf16[1,2,8,32,1024]{4,3,2,1,0:T(8,128)(2,1)}, u32[]{:S(2)}) copy-start(bf16[1,2,8,32,1024]{4,3,2,1,0:T(8,128)(2,1)} %param.13) | copy-start | bytes 3145732
  6.2 1.2 %copy-start.3 = (bf16[1,2,8,32,1024]{4,3,2,1,0:T(8,128)(2,1)S(1)}, bf16[1,2,8,32,1024]{4,3,2,1,0:T(8,128)(2,1)}, u32[]{:S(2)}) copy-start(bf16[1,2,8,32,1024]{4,3,2,1,0:T(8,128)(2,1)} %param.14) | copy-start | bytes 3145732
  7.4 0.8 %copy-start.4 = (bf16[1,8192]{1,0:T(2,128)(2,1)S(1)}, bf16[1,8192]{1,0:T(2,128)(2,1)}, u32[]{:S(2)}) copy-start(bf16[1,8192]{1,0:T(2,128)(2,1)} %gain_hbm.1) | copy-start | bytes 49156
  8.2 0.7 %copy-start.5 = (bf16[1,8,512]{2,1,0:T(8,128)(2,1)S(1)}, bf16[1,8,512]{2,1,0:T(8,128)(2,1)}, u32[]{:S(2)}) copy-start(bf16[1,8,512]{2,1,0:T(8,128)(2,1)} %param.8) | copy-start | bytes 24580
  8.9 0.7 %copy-start.6 = (bf16[1,8,512]{2,1,0:T(8,128)(2,1)S(1)}, bf16[1,8,512]{2,1,0:T(8,128)(2,1)}, u32[]{:S(2)}) copy-start(bf16[1,8,512]{2,1,0:T(8,128)(2,1)} %newcomer_ref.1) | copy-start | bytes 24580
  9.6 0.7 %copy-start.7 = (s32[3,8]{1,0:T(4,128)S(1)}, s32[3,8]{1,0:T(4,128)}, u32[]{:S(2)}) copy-start(s32[3,8]{1,0:T(4,128)} %lengths_ref.1) | copy-start | bytes 292

commit v2 on v1

--- a/solution.py
+++ b/solution.py
@@ -47,6 +47,7 @@
     inputs,
     normed,
     heads,
+    fresh_heads,
     staged,
     parts,
     leaving,
@@ -56,6 +57,8 @@
     cache_sem,
     send_sem,
     recv_sem,
+    heads_sem,
+    ready_sem,
 ):
     ticks, rows, width = out_ref.shape
     features = query_w.shape[0]
@@ -102,8 +105,12 @@
         for load in cache_loads[-1]:
             load.start()
 
+    per_group = GROUP // own_heads
+    own_group = me // per_group
+
     def peer(step):
-        return lax.rem(me + step, n)
+        group = lax.rem(own_group + step // per_group, KVH)
+        return group * per_group + lax.rem(me + step, per_group)
 
     barrier = pltpu.get_barrier_semaphore()
 
@@ -118,34 +125,26 @@
 
         @pl.when(section < sections - 1)
         def _():
-            def greet_next(step, carry):
-                pl.semaphore_signal(
-                    barrier, inc=1, device_id=(section + 1, peer(step)), device_id_type=MESH
-                )
-                return carry
-
-            lax.fori_loop(0, n, greet_next, 0)
+            pl.semaphore_signal(barrier, inc=1, device_id=(section + 1, me), device_id_type=MESH)
 
         @pl.when(section > 0)
         def _():
-            def greet_previous(step, carry):
-                pl.semaphore_signal(
-                    barrier, inc=1, device_id=(section - 1, peer(step)), device_id_type=MESH
-                )
-                return carry
-
-            lax.fori_loop(0, n, greet_previous, 0)
+            pl.semaphore_signal(barrier, inc=1, device_id=(section - 1, me), device_id_type=MESH)
 
     neighbours = (section > 0).astype(jnp.int32) + (section < sections - 1).astype(jnp.int32)
-    pl.semaphore_wait(barrier, n - 1 + n * neighbours)
-
-    def spread(source, target, tick, phase):
+    pl.semaphore_wait(barrier, n - 1 + neighbours)
+    if sections > 1:
+        @pl.when(section > 0)
+        def _():
+            pl.semaphore_signal(ready_sem, inc=1, device_id=(section - 1, me), device_id_type=MESH)
+
+    def spread(source, target, sent, received):
         def send(step, carry):
             pltpu.make_async_remote_copy(
                 src_ref=source,
                 dst_ref=target,
-                send_sem=send_sem.at[tick, phase],
-                recv_sem=recv_sem.at[tick, phase],
+                send_sem=sent,
+                recv_sem=received,
                 device_id=(section, peer(step)),
                 device_id_type=MESH,
             ).start()
@@ -157,7 +156,7 @@
         whole = buffer.at[pl.ds(0, count)]
         pltpu.make_async_copy(whole, whole, sem).wait()
 
-    spread(entering_ref, inputs.at[0, me], 0, 0)
+    spread(entering_ref, inputs.at[0, me], send_sem.at[0, 0], recv_sem.at[0, 0])
 
     @pl.when(section == 0)
     def _():
@@ -165,7 +164,9 @@
             pltpu.make_async_copy(
                 newcomer_ref.at[t - 1], inputs.at[t, me], load_sem.at[1 + t]
             ).start()
-            spread(newcomer_ref.at[t - 1], inputs.at[t, me], t, 0)
+            spread(
+                newcomer_ref.at[t - 1], inputs.at[t, me], send_sem.at[t, 0], recv_sem.at[t, 0]
+            )
 
     lane = lax.broadcasted_iota(jnp.int32, (rows, HD), 1)
     row = lax.broadcasted_iota(jnp.int32, (rows, HD), 0)
@@ -194,6 +195,21 @@
         cosine, sine = turns[t]
         return head * cosine + pltpu.roll(head, half, 1) * sine
 
+    kinds = n // 2
+    fresh_group = (me % kinds) // pieces
+    fresh_slot = (me // kinds) * pieces + me % pieces
+    at_home = fresh_group == own_group
+
+    def fresh_all(tick, sem, count):
+        @pl.when(at_home)
+        def _():
+            if count > 1:
+                arrived(fresh_heads.at[tick], count - 1, sem)
+
+        @pl.when(jnp.logical_not(at_home))
+        def _():
+            arrived(fresh_heads.at[tick], count, sem)
+
     gain_load.wait()
     for t in range(ticks):
         if t == 0:
@@ -232,34 +248,44 @@
                     load.wait()
             query = query + jnp.dot(normed[:, part], query_w[part], preferred_element_type=F32)
             fresh = fresh + jnp.dot(normed[:, part], keyvalue_w[part], preferred_element_type=F32)
-        message = [
-            rotated(query[:, h * HD : (h + 1) * HD], t) for h in range(own_heads)
-        ]
-        fresh = fresh.astype(BF16).astype(F32)
+        heads[t, me] = jnp.concatenate(
+            [rotated(query[:, h * HD : (h + 1) * HD], t) for h in range(own_heads)], axis=0
+        ).astype(BF16)
+        spread(heads.at[t, me], heads.at[t, me], send_sem.at[t, 1], heads_sem.at[t, own_group])
+        fresh = fresh.astype(BF16)
         if pieces > 1:
-            fresh = jnp.concatenate([fresh] * pieces, axis=1)
-            fresh = jnp.where(lane // kv_width == me % pieces, fresh, 0.0)
-        message.append(fresh)
-        spare = heads.shape[2] - own_rows - rows
-        if spare:
-            message.append(jnp.zeros((spare, HD), F32))
-        heads[t, me] = jnp.concatenate(message, axis=0).astype(BF16)
-        spread(heads.at[t, me], heads.at[t, me], t, 1)
+            fresh = jnp.concatenate([fresh.astype(F32)] * pieces, axis=1)
+            fresh = jnp.where(lane // kv_width == me % pieces, fresh, 0.0).astype(BF16)
+        fresh_heads[t, 2 * pieces] = fresh
+        for j in range(per_group):
+            target = fresh_group * per_group + j
+
+            @pl.when(target == me)
+            def _():
+                fresh_heads[t, fresh_slot] = fresh
+
+            @pl.when(target != me)
+            def _():
+                pltpu.make_async_remote_copy(
+                    src_ref=fresh_heads.at[t, 2 * pieces],
+                    dst_ref=fresh_heads.at[t, fresh_slot],
+                    send_sem=send_sem.at[t, 4],
+                    recv_sem=recv_sem.at[t, 1],
+                    device_id=(section, target),
+                    device_id_type=MESH,
+                ).start()
 
         for load in cache_loads[t]:
             load.wait()
-        arrived(heads.at[t], n - 1, recv_sem.at[t, 1])
         valid = masks[t]
-        per_group = GROUP // own_heads
-        for g in range(KVH):
+        for k in range(KVH):
+            g = lax.rem(own_group + KVH - k, KVH)
+            if k > 0 or per_group > 1:
+                arrived(heads.at[t], per_group - (k == 0), heads_sem.at[t, g])
             grouped = jnp.concatenate(
-                [
-                    heads[t, g * per_group + j].astype(F32)[:own_rows]
-                    for j in range(per_group)
-                ],
-                axis=0,
+                [heads[t, g * per_group + j].astype(F32) for j in range(per_group)], axis=0
             ).astype(BF16)
-            part = pl.ds(g * HD, HD)
+            part = pl.ds(pl.multiple_of(g * HD, HD), HD)
             scores = lax.dot_general(
                 keys[t, :, part],
                 grouped,
@@ -282,18 +308,12 @@
             stats = jnp.concatenate([stats, jnp.zeros((8, HD - group_rows), F32)], axis=1)
             for j in range(per_group):
                 target = g * per_group + j
-                message = [weighted[j * own_rows : (j + 1) * own_rows], stats]
-                if spare:
-                    message.append(jnp.zeros((spare, HD), F32))
-                message = jnp.concatenate(message, axis=0).astype(BF16)
+                message = jnp.concatenate(
+                    [weighted[j * own_rows : (j + 1) * own_rows], stats], axis=0
+                ).astype(BF16)
                 staged[t, target] = message
 
-                @pl.when(target == me)
-                def _():
-                    parts[t, me] = message
-
-                @pl.when(target != me)
-                def _():
+                def send():
                     pltpu.make_async_remote_copy(
                         src_ref=staged.at[t, target],
                         dst_ref=parts.at[t, me],
@@ -303,18 +323,25 @@
                         device_id_type=MESH,
                     ).start()
 
-        group = (me * own_heads) // GROUP
+                if k > 0:
+                    send()
+                else:
+
+                    @pl.when(target == me)
+                    def _():
+                        parts[t, me] = message
+
+                    pl.when(target != me)(send)
+
+        fresh_all(t, recv_sem.at[t, 1], 2 * pieces)
         new_key = jnp.zeros((rows, HD), F32)
         new_value = jnp.zeros((rows, HD), F32)
         for j in range(pieces):
-            new_key = new_key + heads[t, group * pieces + j].astype(F32)[own_rows : own_rows + rows]
-            new_value = (
-                new_value
-                + heads[t, n // 2 + group * pieces + j].astype(F32)[own_rows : own_rows + rows]
-            )
+            new_key = new_key + fresh_heads[t, j].astype(F32)
+            new_value = new_value + fresh_heads[t, pieces + j].astype(F32)
         new_key = jnp.concatenate([rotated(new_key, t)] * own_heads, axis=0)
         new_value = jnp.concatenate([new_value] * own_heads, axis=0)
-        own_query = heads[t, me].astype(F32)[:own_rows]
+        own_query = heads[t, me].astype(F32)
         new_score = jnp.sum(own_query * new_key, axis=-1, keepdims=True) * scale
 
         arrived(parts.at[t], n - 1, recv_sem.at[t, 2])
@@ -351,6 +378,9 @@
 
             @pl.when(section < sections - 1)
             def _():
+                if t == 0:
+                    pl.semaphore_wait(ready_sem, 1)
+
                 def send(step, carry):
                     pltpu.make_async_remote_copy(
                         src_ref=leaving.at[t],
@@ -374,6 +404,7 @@
                 arrived(inputs.at[t], n - 1, send_sem.at[t, 0])
 
         arrived(heads.at[t], n - 1, send_sem.at[t, 1])
+        fresh_all(t, send_sem.at[t, 4], per_group)
         arrived(parts.at[t], n - 1, send_sem.at[t, 2])
         if t < ticks - 1 and sections > 1:
 
@@ -399,7 +430,9 @@
     kv_width = keyvalue_weight.shape[2]
     _, ticks, _, span, kv_features = key_cache.shape
     own_rows = (NH // n) * rows
-    message_rows = -(-(own_rows + 8) // 16) * 16
+    message_rows = own_rows + 8
+    pieces = HD // kv_width
+    slots = max(2 * pieces + 1, NH // KVH * n // NH)
     chunks = 4
     anywhere = pl.BlockSpec(memory_space=pl.ANY)
     out = pl.pallas_call(
@@ -415,7 +448,8 @@
             pltpu.VMEM((1, features), BF16),
             pltpu.VMEM((ticks, n, rows, width), BF16),
             pltpu.VMEM((rows, features), BF16),
-            pltpu.VMEM((ticks, n, message_rows, HD), BF16),
+            pltpu.VMEM((ticks, n, own_rows, HD), BF16),
+            pltpu.VMEM((ticks, slots, rows, HD), BF16),
             pltpu.VMEM((ticks, n, message_rows, HD), BF16),
             pltpu.VMEM((ticks, n, message_rows, HD), BF16),
             pltpu.VMEM((ticks, rows, width), BF16),
@@ -423,11 +457,13 @@
             pltpu.SemaphoreType.DMA((1 + ticks,)),
             pltpu.SemaphoreType.DMA((chunks, 2)),
             pltpu.SemaphoreType.DMA((ticks, 2)),
-            pltpu.SemaphoreType.DMA((ticks, 4)),
+            pltpu.SemaphoreType.DMA((ticks, 5)),
             pltpu.SemaphoreType.DMA((ticks, 3)),
+            pltpu.SemaphoreType.DMA((ticks, KVH)),
+            pltpu.SemaphoreType.REGULAR,
         ],
         compiler_params=pltpu.CompilerParams(
-            collective_id=0, has_side_effects=True, vmem_limit_bytes=40 << 20
+            collective_id=0, has_side_effects=True, vmem_limit_bytes=60 << 20
         ),
     )(
         cache_lengths,

time: 60.8 us -> 47.2 us (0.78); the launches traced: 59.9 us -> 46.9 us
  local copies, waits for them, and re-layouts: 10.9 us -> 1.32 us
  Pallas kernels: 49 us -> 45.6 us
    unnamed x17 -> x1, local copies, waits for them, and re-layouts: 10.9 us -> 1.32 us
    pallas_call x1, Pallas kernels: 49 us -> 45.6 us  [shards(): pl.pallas_call(functools.partial(layer_kernel, n, sections), out_shape=ja...]
where the time goes in v2:
time: 47.2 us; the launch traced here: 46.9 us
  Pallas kernels  45.6 us (97%)
  local copies, waits for them, and re-layouts  1.32 us (3%)
    pallas_call x1, Pallas kernels, shards(): pl.pallas_call(functools.partial(layer_kernel, n, sections), out_shape=ja...  45.6 us
    unnamed x1, local copies, waits for them, and re-layouts  1.32 us

profile of v2, /device:TPU:3, one launch (start us, length us, event | category | flops | bytes accessed | tf_op | source)
XLA Modules:
  0.0 46.9 jit_solution(15968914610806715156)
XLA Ops:
  0.0 45.6 %shard_map.82 = bf16[2,8,512]{2,1,0:T(8,128)(2,1)} custom-call(s32[3,8]{1,0:T(4,128)} %lengths_ref.1, bf16[8,512]{1,0:T(8,128)(2,1)} %bitcast.11, bf16[1,8,512]{2,1,0:T(8,128)(2,1)} %newcomer_ref.1, bf16[1,8192]{1,0:T(2,128)(2,1)} %gain_hbm.1, bf16[8192,512]{1,0:T(8,128)(2,1)} %bitcast.6, bf16[8192,128]{1,0:T(8,128)(2,1)} %bitcast.7, ...), custom_call_target="tpu_custom_call" | custom-call | tf_op jit(solution)/shard_map/pallas_call | solution.py:438
  45.6 1.3 %copy.10 = bf16[1,2,8,512]{3,2,1,0:T(8,128)(2,1)} copy(bf16[1,2,8,512]{3,2,1,0:T(8,128)(2,1)} %bitcast.10) | data formatting | bytes 32768

commit v3 on v2

--- a/solution.py
+++ b/solution.py
@@ -12,6 +12,7 @@
 KVH = 8
 HD = 128
 GROUP = NH // KVH
+PAIRS = KVH // 2
 THETA = 500000.0
 EPS = 1e-05
 NEG = -1e30
@@ -67,6 +68,7 @@
     kv_width = keyvalue_w.shape[1]
     pieces = HD // kv_width
     group_rows = GROUP * rows
+    pair_rows = 2 * group_rows
     span = keys.shape[1] // rows
     chunks = weight_sem.shape[0]
     depth = features // chunks
@@ -108,9 +110,12 @@
     per_group = GROUP // own_heads
     own_group = me // per_group
 
+    per_pair = 2 * per_group
+    own_pair = me // per_pair
+
     def peer(step):
-        group = lax.rem(own_group + step // per_group, KVH)
-        return group * per_group + lax.rem(me + step, per_group)
+        pair = lax.rem(own_pair + step // per_pair, PAIRS)
+        return pair * per_pair + lax.rem(me + step, per_pair)
 
     barrier = pltpu.get_barrier_semaphore()
 
@@ -175,13 +180,13 @@
     frequency = jnp.exp(exponent * (-math.log(THETA)))
     turns = []
     masks = []
-    place = lax.broadcasted_iota(jnp.int32, (rows * span, group_rows), 0)
-    column = lax.broadcasted_iota(jnp.int32, (rows * span, group_rows), 1)
+    place = lax.broadcasted_iota(jnp.int32, (rows * span, pair_rows), 0)
+    column = lax.broadcasted_iota(jnp.int32, (rows * span, pair_rows), 1)
     position = me * span + place % span
     for t in range(ticks):
         micro = t + sections - 1 - section
         by_row = jnp.zeros((rows, HD), jnp.int32)
-        limit = jnp.zeros((rows * span, group_rows), jnp.int32)
+        limit = jnp.zeros((rows * span, pair_rows), jnp.int32)
         for b in range(rows):
             length = lengths_ref[micro, b]
             by_row = jnp.where(row == b, length, by_row)
@@ -240,18 +245,21 @@
             normed[:, part] = (x * factor * gain[:, part].astype(F32)).astype(BF16)
 
         query = jnp.zeros((rows, width), F32)
+        for c in range(chunks):
+            part = pl.ds(c * depth, depth)
+            if t == 0:
+                weight_loads[c][0].wait()
+            query = query + jnp.dot(normed[:, part], query_w[part], preferred_element_type=F32)
+        heads[t, me] = jnp.concatenate(
+            [rotated(query[:, h * HD : (h + 1) * HD], t) for h in range(own_heads)], axis=0
+        ).astype(BF16)
+        spread(heads.at[t, me], heads.at[t, me], send_sem.at[t, 1], heads_sem.at[t, own_pair])
         fresh = jnp.zeros((rows, kv_width), F32)
         for c in range(chunks):
             part = pl.ds(c * depth, depth)
             if t == 0:
-                for load in weight_loads[c]:
-                    load.wait()
-            query = query + jnp.dot(normed[:, part], query_w[part], preferred_element_type=F32)
+                weight_loads[c][1].wait()
             fresh = fresh + jnp.dot(normed[:, part], keyvalue_w[part], preferred_element_type=F32)
-        heads[t, me] = jnp.concatenate(
-            [rotated(query[:, h * HD : (h + 1) * HD], t) for h in range(own_heads)], axis=0
-        ).astype(BF16)
-        spread(heads.at[t, me], heads.at[t, me], send_sem.at[t, 1], heads_sem.at[t, own_group])
         fresh = fresh.astype(BF16)
         if pieces > 1:
             fresh = jnp.concatenate([fresh.astype(F32)] * pieces, axis=1)
@@ -278,17 +286,20 @@
         for load in cache_loads[t]:
             load.wait()
         valid = masks[t]
-        for k in range(KVH):
-            g = lax.rem(own_group + KVH - k, KVH)
-            if k > 0 or per_group > 1:
-                arrived(heads.at[t], per_group - (k == 0), heads_sem.at[t, g])
-            grouped = jnp.concatenate(
-                [heads[t, g * per_group + j].astype(F32) for j in range(per_group)], axis=0
+        upper = lax.broadcasted_iota(jnp.int32, (pair_rows, HD), 0) < group_rows
+        for k in range(PAIRS):
+            pair = lax.rem(own_pair + PAIRS - k, PAIRS)
+            arrived(heads.at[t], per_pair - (k == 0), heads_sem.at[t, pair])
+            both = jnp.concatenate(
+                [heads[t, pair * per_pair + j].astype(F32) for j in range(per_pair)], axis=0
+            )
+            both = jnp.concatenate(
+                [jnp.where(upper, both, 0.0), jnp.where(upper, 0.0, both)], axis=1
             ).astype(BF16)
-            part = pl.ds(pl.multiple_of(g * HD, HD), HD)
+            part = pl.ds(pl.multiple_of(pair * 2 * HD, 2 * HD), 2 * HD)
             scores = lax.dot_general(
                 keys[t, :, part],
-                grouped,
+                both,
                 (((1,), (1,)), ((), ())),
                 preferred_element_type=F32,
             )
@@ -302,12 +313,12 @@
                 (((0,), (0,)), ((), ())),
                 preferred_element_type=F32,
             )
+            weighted = jnp.where(upper, weighted[:, :HD], weighted[:, HD:])
             stats = jnp.concatenate(
-                three_parts(top) + three_parts(total) + [jnp.zeros((2, group_rows), F32)], axis=0
-            )
-            stats = jnp.concatenate([stats, jnp.zeros((8, HD - group_rows), F32)], axis=1)
-            for j in range(per_group):
-                target = g * per_group + j
+                three_parts(top) + three_parts(total) + [jnp.zeros((2, pair_rows), F32)], axis=0
+            )
+            for j in range(per_pair):
+                target = pair * per_pair + j
                 message = jnp.concatenate(
                     [weighted[j * own_rows : (j + 1) * own_rows], stats], axis=0
                 ).astype(BF16)
@@ -356,7 +367,7 @@
         totals = jnp.concatenate(totals + [jnp.zeros((blank, HD), F32)], axis=0)
         columns[0] = tops.T
         columns[1] = totals.T
-        first = pl.multiple_of((me % per_group) * own_rows, 8)
+        first = pl.multiple_of((me % per_pair) * own_rows, 8)
         tops = columns[0, pl.ds(first, own_rows), :]
         totals = columns[1, pl.ds(first, own_rows), :]
         top = jnp.maximum(jnp.max(tops, axis=-1, keepdims=True), new_score)
@@ -459,7 +470,7 @@
             pltpu.SemaphoreType.DMA((ticks, 2)),
             pltpu.SemaphoreType.DMA((ticks, 5)),
             pltpu.SemaphoreType.DMA((ticks, 3)),
-            pltpu.SemaphoreType.DMA((ticks, KVH)),
+            pltpu.SemaphoreType.DMA((ticks, PAIRS)),
             pltpu.SemaphoreType.REGULAR,
         ],
         compiler_params=pltpu.CompilerParams(

time: 47.2 us -> 47 us (level)
  no operation moved by 1% of the time
where the time goes in v3:
time: 47 us; the launch traced here: 46.8 us
  Pallas kernels  45.4 us (97%)
  local copies, waits for them, and re-layouts  1.32 us (3%)
    pallas_call x1, Pallas kernels, shards(): pl.pallas_call(functools.partial(layer_kernel, n, sections), out_shape=ja...  45.4 us
    unnamed x1, local copies, waits for them, and re-layouts  1.32 us

profile of v3, /device:TPU:3, one launch (start us, length us, event | category | flops | bytes accessed | tf_op | source)
XLA Modules:
  0.0 46.8 jit_solution(10287283510914058670)
XLA Ops:
  0.0 45.4 %shard_map.82 = bf16[2,8,512]{2,1,0:T(8,128)(2,1)} custom-call(s32[3,8]{1,0:T(4,128)} %lengths_ref.1, bf16[8,512]{1,0:T(8,128)(2,1)} %bitcast.11, bf16[1,8,512]{2,1,0:T(8,128)(2,1)} %newcomer_ref.1, bf16[1,8192]{1,0:T(2,128)(2,1)} %gain_hbm.1, bf16[8192,512]{1,0:T(8,128)(2,1)} %bitcast.6, bf16[8192,128]{1,0:T(8,128)(2,1)} %bitcast.7, ...), custom_call_target="tpu_custom_call" | custom-call | tf_op jit(solution)/shard_map/pallas_call | solution.py:449
  45.4 1.3 %copy.10 = bf16[1,2,8,512]{3,2,1,0:T(8,128)(2,1)} copy(bf16[1,2,8,512]{3,2,1,0:T(8,128)(2,1)} %bitcast.10) | data formatting | bytes 32768

commit v4 on v3

--- a/solution.py
+++ b/solution.py
@@ -155,7 +155,8 @@
             ).start()
             return carry
 
-        lax.fori_loop(1, n, send, 0)
+        lax.fori_loop(per_pair, n, send, 0)
+        lax.fori_loop(1, per_pair, send, 0)
 
     def arrived(buffer, count, sem):
         whole = buffer.at[pl.ds(0, count)]
@@ -287,7 +288,7 @@
             load.wait()
         valid = masks[t]
         upper = lax.broadcasted_iota(jnp.int32, (pair_rows, HD), 0) < group_rows
-        for k in range(PAIRS):
+        for k in [*range(1, PAIRS), 0]:
             pair = lax.rem(own_pair + PAIRS - k, PAIRS)
             arrived(heads.at[t], per_pair - (k == 0), heads_sem.at[t, pair])
             both = jnp.concatenate(

time: 47 us -> 46.9 us (level)
  no operation moved by 1% of the time
where the time goes in v4:
time: 46.9 us; the launch traced here: 46.7 us
  Pallas kernels  45.4 us (97%)
  local copies, waits for them, and re-layouts  1.32 us (3%)
    pallas_call x1, Pallas kernels, shards(): pl.pallas_call(functools.partial(layer_kernel, n, sections), out_shape=ja...  45.4 us
    unnamed x1, local copies, waits for them, and re-layouts  1.32 us

profile of v4, /device:TPU:3, one launch (start us, length us, event | category | flops | bytes accessed | tf_op | source)
XLA Modules:
  0.0 46.7 jit_solution(2329124930094717739)
XLA Ops:
  0.0 45.4 %shard_map.82 = bf16[2,8,512]{2,1,0:T(8,128)(2,1)} custom-call(s32[3,8]{1,0:T(4,128)} %lengths_ref.1, bf16[8,512]{1,0:T(8,128)(2,1)} %bitcast.11, bf16[1,8,512]{2,1,0:T(8,128)(2,1)} %newcomer_ref.1, bf16[1,8192]{1,0:T(2,128)(2,1)} %gain_hbm.1, bf16[8192,512]{1,0:T(8,128)(2,1)} %bitcast.6, bf16[8192,128]{1,0:T(8,128)(2,1)} %bitcast.7, ...), custom_call_target="tpu_custom_call" | custom-call | tf_op jit(solution)/shard_map/pallas_call | solution.py:450
  45.4 1.3 %copy.10 = bf16[1,2,8,512]{3,2,1,0:T(8,128)(2,1)} copy(bf16[1,2,8,512]{3,2,1,0:T(8,128)(2,1)} %bitcast.10) | data formatting | bytes 32768

commit v5 on v3

--- a/solution.py
+++ b/solution.py
@@ -169,9 +169,6 @@
             pltpu.make_async_copy(
                 newcomer_ref.at[t - 1], inputs.at[t, me], load_sem.at[1 + t]
             ).start()
-            spread(
-                newcomer_ref.at[t - 1], inputs.at[t, me], send_sem.at[t, 0], recv_sem.at[t, 0]
-            )
 
     lane = lax.broadcasted_iota(jnp.int32, (rows, HD), 1)
     row = lax.broadcasted_iota(jnp.int32, (rows, HD), 0)
@@ -356,6 +353,16 @@
         new_score = jnp.sum(own_query * new_key, axis=-1, keepdims=True) * scale
 
         arrived(parts.at[t], n - 1, recv_sem.at[t, 2])
+        if t < ticks - 1:
+            @pl.when(section == 0)
+            def _():
+                spread(
+                    newcomer_ref.at[t],
+                    inputs.at[t + 1, me],
+                    send_sem.at[t + 1, 0],
+                    recv_sem.at[t + 1, 0],
+                )
+
         tops = []
         totals = []
         for s in range(n):

time: 47 us -> 47.8 us (1.017)
  Pallas kernels: 45.4 us -> 46.2 us
    pallas_call x1, Pallas kernels: 45.4 us -> 46.2 us  [shards(): pl.pallas_call(functools.partial(layer_kernel, n, sections), out_shape=ja...]
where the time goes in v5:
time: 47.8 us; the launch traced here: 47.5 us
  Pallas kernels  46.2 us (97%)
  local copies, waits for them, and re-layouts  1.32 us (3%)
    pallas_call x1, Pallas kernels, shards(): pl.pallas_call(functools.partial(layer_kernel, n, sections), out_shape=ja...  46.2 us
    unnamed x1, local copies, waits for them, and re-layouts  1.32 us

profile of v5, /device:TPU:3, one launch (start us, length us, event | category | flops | bytes accessed | tf_op | source)
XLA Modules:
  0.0 47.5 jit_solution(2844980373687129116)
XLA Ops:
  0.0 46.2 %shard_map.82 = bf16[2,8,512]{2,1,0:T(8,128)(2,1)} custom-call(s32[3,8]{1,0:T(4,128)} %lengths_ref.1, bf16[8,512]{1,0:T(8,128)(2,1)} %bitcast.11, bf16[1,8,512]{2,1,0:T(8,128)(2,1)} %newcomer_ref.1, bf16[1,8192]{1,0:T(2,128)(2,1)} %gain_hbm.1, bf16[8192,512]{1,0:T(8,128)(2,1)} %bitcast.6, bf16[8192,128]{1,0:T(8,128)(2,1)} %bitcast.7, ...), custom_call_target="tpu_custom_call" | custom-call | tf_op jit(solution)/shard_map/pallas_call | solution.py:456
  46.2 1.3 %copy.10 = bf16[1,2,8,512]{3,2,1,0:T(8,128)(2,1)} copy(bf16[1,2,8,512]{3,2,1,0:T(8,128)(2,1)} %bitcast.10) | data formatting | bytes 32768
